TPU v7x, 512 devices: a whole 4x4x16 slice. The times are simulated.
512 devices in a mesh: req: 64 (over x, z), tp: 8 (over y, core).
Axes of the slice: x: 4, y: 4, z: 16, core: 2. Of those that a mesh axis runs over, the one named last changes fastest.
Arguments:
- hidden: bfloat16 [8192, 1280], P(('req', 'tp')), may hold values from -6 to 6
- gate_weight: bfloat16 [1280, 4096], P(None, 'tp'), may hold values from -0.15625 to 0.15625
- up_weight: bfloat16 [1280, 4096], P(None, 'tp'), may hold values from -0.15625 to 0.15625
- down_weight: bfloat16 [4096, 1280], P('tp'), may hold values from -0.09375 to 0.09375
- gate_scale: float32 [4096], P('tp'), may hold values from 0.1 to 1.9
- up_scale: float32 [4096], P('tp'), may hold values from 0.1 to 1.9
- update_step_size: float32 [1280], replicated, may hold values from 0.05 to 0.6
- adapter_down_maps: bfloat16 [64, 1280, 16], P('req'), may hold values from -0.15625 to 0.15625
- adapter_up_maps: bfloat16 [64, 16, 4096], P('req', None, 'tp'), may hold values from -1.5 to 1.5
- lengths: int32 [512], P('req'), may hold values from 9 to 16, as said below
- request_adapter_index: int32 [512], P('req'), may hold values from 0 to 63, as said below
Outputs:
- updated: bfloat16 [8192, 1280], P(('req', 'tp'))
Inputs may be any that keep to these rules, and one draw needn't show every extreme that they name: `request_adapter_index`: among the 8 requests of one index of req no adapter id occurs more than 1 times; one adapter occurs exactly 1 times on every index of req. `lengths`: on every index of req some request has length 16: those served by the adapter that every index uses.
All inputs are finite; a program needn't handle non-finite values.
Results may differ from a plain program's by a relative error of at most 0.003.
Values may be sent and summed in bfloat16 or wider, within the bound.
A program may use at most 64 MiB of HBM per device.

v0:
```python
import jax
import jax.numpy as jnp
from jax import lax
from jax.sharding import PartitionSpec as P


def rms_norm(values):
    return values * lax.rsqrt(jnp.mean(values * values, axis=-1, keepdims=True) + 1e-06)


def body(
    hidden,
    gate_weight,
    up_weight,
    down_weight,
    gate_scale,
    up_scale,
    update_step_size,
    adapter_down_maps,
    adapter_up_maps,
    lengths,
    request_adapter_index,
):
    gathered = lax.all_gather(hidden, "tp", axis=0, tiled=True)
    seq_count = lengths.shape[0]
    token_count = gathered.shape[0]
    pad_length = token_count // seq_count
    features = gathered.shape[1]
    live_mask = jnp.arange(pad_length)[None, :] < lengths[:, None]
    masked = gathered.reshape(seq_count, pad_length, features) * live_mask[:, :, None].astype(
        jnp.bfloat16
    )
    owners = lax.axis_size("req")
    per_owner = max(1, seq_count // owners)
    owner_match = request_adapter_index[None, :] == jnp.arange(owners)[:, None]
    match_int = owner_match.astype(jnp.int32)
    slot_rank = jnp.sum(match_int * (jnp.cumsum(match_int, axis=1) - 1), axis=0)
    slot_match = owner_match[:, None, :] & (
        slot_rank[None, None, :] == jnp.arange(per_owner)[None, :, None]
    )
    dispatch = slot_match.reshape(owners * per_owner, seq_count).astype(jnp.bfloat16)
    request_down_map = adapter_down_maps[0]
    request_up_map = adapter_up_maps[0]
    tp_count = lax.axis_size("tp")
    tp_index = lax.axis_index("tp")
    outgoing = jnp.einsum(
        "cs,sjd->cjd", dispatch, masked, preferred_element_type=jnp.float32
    ).astype(jnp.bfloat16)
    shrink = jnp.einsum(
        "sjd,dr->sjr",
        lax.all_to_all(outgoing, "req", split_axis=0, concat_axis=0, tiled=True),
        request_down_map,
        preferred_element_type=jnp.float32,
    ).astype(jnp.bfloat16)
    delta = jnp.einsum(
        "sjr,rf->sjf", shrink, request_up_map, preferred_element_type=jnp.float32
    ).astype(jnp.bfloat16)
    returned = lax.all_to_all(delta, "req", split_axis=0, concat_axis=0, tiled=True)
    delta_home = jnp.einsum(
        "cs,cjf->sjf", dispatch, returned, preferred_element_type=jnp.float32
    ).astype(jnp.bfloat16)
    delta_rows = delta_home.reshape(token_count, delta_home.shape[2]).astype(jnp.float32)
    gate_pre = jnp.dot(gathered, gate_weight, preferred_element_type=jnp.float32) * gate_scale
    up_pre = (
        jnp.dot(gathered, up_weight, preferred_element_type=jnp.float32) + 0.5 * delta_rows
    ) * up_scale
    hidden_units = (jax.nn.silu(gate_pre) * up_pre).astype(jnp.bfloat16)
    row_share = token_count // tp_count
    row_start = tp_index * row_share
    branch = lax.psum_scatter(
        jnp.dot(hidden_units, down_weight, preferred_element_type=jnp.float32),
        "tp",
        scatter_dimension=0,
        tiled=True,
    )
    start_state = rms_norm(hidden.astype(jnp.float32))
    blended = start_state + update_step_size * (rms_norm(branch) - start_state)
    live_rows = lax.dynamic_slice_in_dim(
        live_mask.reshape(token_count).astype(jnp.float32), row_start, row_share, 0
    )
    return (rms_norm(blended) * live_rows[:, None]).astype(jnp.bfloat16)


def solution(mesh):
    placed = (
        P(("req", "tp"), None),
        P(None, "tp"),
        P(None, "tp"),
        P("tp", None),
        P("tp"),
        P("tp"),
        P(),
        P("req", None, None),
        P("req", None, "tp"),
        P("req"),
        P("req"),
    )
    return jax.shard_map(
        body, mesh=mesh, in_specs=placed, out_specs=P(("req", "tp"), None), check_vma=False
    )
```

profile of v0, /device:TPU:1, one launch (start us, length us, event | category | flops | bytes accessed | tf_op | source)
XLA Modules:
  0.0 275.1 jit_solution(13446137086280386212)
XLA Ops:
  6.5 0.0 copy-start
  6.5 0.8 fusion.23
  7.4 19.8 %all_gather.3 = bf16[128,1280]{1,0:T(8,128)(2,1)S(1)} all-gather(bf16[16,1280]{1,0:T(8,128)(2,1)} %param.11), channel_id=1, replica_groups=mesh['req'=64,'tp'=8] {'tp'}, dimensions={0}, use_global_device_ids=true | all-gather | bytes 368640 | tf_op jit(solution)/shard_map/all_gather | solution.py:24
  27.1 0.1 reshape.133
  27.2 0.7 fusion.26
  28.0 0.8 select_reduce_fusion
  28.8 0.1 broadcast_multiply_fusion
  28.9 1.6 convolution_convert_fusion
  30.5 1.4 copy.21
  32.0 0.0 copy-start.7
  32.0 133.5 %all_to_all.10 = bf16[64,16,1280]{2,1,0:T(8,128)(2,1)S(1)} all-to-all(bf16[64,16,1280]{2,1,0:T(8,128)(2,1)S(1)} %copy.21), channel_id=1, replica_groups=mesh['req'=64,'tp'=8] {'req'}, dimensions={0} | all-to-all | bytes 5242880 | tf_op jit(solution)/shard_map/all_to_all | solution.py:51
  165.5 0.0 copy-done.7
  165.5 0.0 copy-start.3
  165.5 0.8 fusion.20
  166.3 0.3 copy.27
  166.5 0.0 copy-done.3
  166.5 0.5 convolution_convert_fusion.1
  167.0 1.6 copy.23
  168.6 0.0 copy-start.6
  168.6 7.7 %all-to-all-start.1 = ((bf16[64,16,512]{2,1,0:T(8,128)(2,1)}), bf16[64,16,512]{2,1,0:T(8,128)(2,1)S(1)}, u32[]{:S(2)}, u32[]{:S(2)}) async-start(bf16[64,16,512]{2,1,0:T(8,128)(2,1)} %copy.23), calls=%async_computation.1 | async-start | bytes 2097152 | tf_op jit(solution)/shard_map/all_to_all | solution.py:58
  176.3 0.0 copy-start.4
  176.3 0.0 reduce-scatter.2.cloned.1.call-start
  176.3 0.0 copy-done.6
  176.3 1.7 convolution_multiply_fusion
  178.0 0.0 copy-start.5
  178.0 48.1 %all-to-all-done.1 = bf16[64,16,512]{2,1,0:T(8,128)(2,1)S(1)} async-done(((bf16[64,16,512]{2,1,0:T(8,128)(2,1)}), bf16[64,16,512]{2,1,0:T(8,128)(2,1)S(1)}, u32[]{:S(2)}, u32[]{:S(2)}) %all-to-all-start.1) | async-done | bytes 1048608 | tf_op jit(solution)/shard_map/all_to_all | solution.py:58
  226.1 0.0 copy-done.4
  226.1 1.2 fusion.4
  227.3 0.2 copy.25
  227.5 0.0 copy-done
  227.5 0.0 copy-done.5
  227.5 0.0 copy-start.1
  227.5 0.0 copy-start.2
  227.6 2.8 %fusion.5 = f32[128,1280]{1,0:T(8,128)} fusion(bf16[512,1280]{1,0:T(8,128)(2,1)S(1)} %copy-done, f32[128,512]{1,0:T(8,128)S(1)} %bitcast.26, bf16[128,1280]{1,0:T(8,128)(2,1)S(1)} %all_gather.3, bf16[1280,512]{1,0:T(8,128)(2,1)} %param.13, f32[128,512]{1,0:T(8,128)S(1)} %convolution_multiply_fusion, f32[512]{0:T(512)S(1)} %copy-done.5), kind=kOutput, calls=%fused_computation.10 | convolution fusion | flops 336068608 | bytes 4130816 | tf_op jit(solution)/shard_map/dot_general | solution.py:71
  230.4 0.0 reduce-scatter.2.cloned.1.call-update
  230.4 0.1 reshape.134
  230.5 0.1 dynamic_slice.3
  230.6 0.0 copy-done.1
  230.6 0.1 fusion.18
  230.7 33.8 %reduce-scatter.2.cloned.1.call-done = f32[16,1280]{1,0:T(8,128)} async-done(((f32[128,1280]{1,0:T(8,128)}), f32[16,1280]{1,0:T(8,128)}) %reduce-scatter.2.cloned.1.call-update) | async-done | bytes 81936 | tf_op jit(solution)/shard_map/reduce_scatter | solution.py:70
  264.5 1.0 multiply_reduce_fusion.1
  265.5 0.0 copy-done.2
  265.5 1.1 multiply_reduce_fusion
  266.6 1.6 multiply_convert_fusion
  (5 shorter events, 0.1 us)
Async XLA Ops:
  6.5 221.0 %copy-start = (bf16[512,1280]{1,0:T(8,128)(2,1)S(1)}, bf16[512,1280]{1,0:T(8,128)(2,1)}, u32[]{:S(2)}) copy-start(bf16[512,1280]{1,0:T(8,128)(2,1)} %param.14) | copy-start | bytes 3932164
  32.0 133.5 %copy-start.7 = (bf16[1,1280,16]{1,2,0:T(8,128)(2,1)S(1)}, bf16[1,1280,16]{1,2,0:T(8,128)(2,1)}, u32[]{:S(2)}) copy-start(bf16[1,1280,16]{1,2,0:T(8,128)(2,1)} %param.18) | copy-start | bytes 122884
  165.5 1.1 copy-start.3
  168.6 7.8 %copy-start.6 = (f32[512]{0:T(512)S(1)}, f32[512]{0:T(512)}, u32[]{:S(2)}) copy-start(f32[512]{0:T(512)} %param.15) | copy-start | bytes 6148
  168.6 57.6 %all-to-all-start.1 = ((bf16[64,16,512]{2,1,0:T(8,128)(2,1)}), bf16[64,16,512]{2,1,0:T(8,128)(2,1)S(1)}, u32[]{:S(2)}, u32[]{:S(2)}) async-start(bf16[64,16,512]{2,1,0:T(8,128)(2,1)} %copy.23), calls=%async_computation.1 | async-start | bytes 2097152 | tf_op jit(solution)/shard_map/all_to_all | solution.py:58
  176.3 49.9 %copy-start.4 = (s32[8]{0:T(128)S(1)}, s32[8]{0:T(128)}, u32[]{:S(2)}) copy-start(s32[8]{0:T(128)} %param.21) | copy-start | bytes 100
  176.3 88.2 %reduce-scatter.2.cloned.1.call-start = ((), (), s32[]{:S(2)}) async-start(), calls=%async_computation.3 | async-start | bytes 737280 | tf_op jit(solution)/shard_map/reduce_scatter | solution.py:70
  178.0 49.5 %copy-start.5 = (f32[512]{0:T(512)S(1)}, f32[512]{0:T(512)}, u32[]{:S(2)}) copy-start(f32[512]{0:T(512)} %param.16) | copy-start | bytes 6148
  227.5 3.0 %copy-start.1 = (bf16[16,1280]{1,0:T(8,128)(2,1)S(1)}, bf16[16,1280]{1,0:T(8,128)(2,1)}, u32[]{:S(2)}) copy-start(bf16[16,1280]{1,0:T(8,128)(2,1)} %param.11) | copy-start | bytes 122884
  227.5 38.0 %copy-start.2 = (f32[1280]{0:T(1024)S(1)}, f32[1280]{0:T(1024)}, u32[]{:S(2)}) copy-start(f32[1280]{0:T(1024)} %param.17) | copy-start | bytes 15364
Sparse Core Ops, SparseCore 0:
  230.5 33.9 reduce-scatter.1
where the time goes:
time: 276 us; the launch traced here: 275 us
  blocking collectives  153 us (55%)
  waiting for transfers between devices  81.9 us (30%)
  between operations  13.5 us (5%)
  matrix products  8.58 us (3%)
  starting transfers between devices  7.73 us (3%)
  other arithmetic  6.37 us (2%)
  local copies, waits for them, and re-layouts  3.72 us (1%)
    all_to_all x1, blocking collectives, body(): lax.all_to_all(outgoing, 'req', split_axis=0, concat_axis=0, tiled=True)  133 us
    all_to_all x1, waiting for transfers between devices, body(): lax.all_to_all(delta, 'req', split_axis=0, concat_axis=0, tiled=True)  48.1 us
    reduce_scatter x1, waiting for transfers between devices, body(): lax.psum_scatter(jnp.dot(hidden_units, down_weight, preferred_element_typ...  33.8 us
    all_gather x1, blocking collectives, body(): gathered = lax.all_gather(hidden, 'tp', axis=0, tiled=True)  19.8 us
    all_to_all x1, starting transfers between devices, body(): lax.all_to_all(delta, 'req', split_axis=0, concat_axis=0, tiled=True)  7.69 us
  transfers between devices with their start and end apart: 2, of which 2 were waited for; matrix products, arithmetic and copies ran while one was open for 1% of the time, Pallas kernels for 0%

commit v1 on v0

v1 whole, which is shorter than its diff:
```python
import jax
import jax.numpy as jnp
from jax import lax
from jax.sharding import PartitionSpec as P


def rms_norm(values):
    return values * lax.rsqrt(jnp.mean(values * values, axis=-1, keepdims=True) + 1e-06)


def body(
    hidden,
    gate_weight,
    up_weight,
    down_weight,
    gate_scale,
    up_scale,
    update_step_size,
    adapter_down_maps,
    adapter_up_maps,
    lengths,
    request_adapter_index,
):
    owners = lax.axis_size("req")
    tp_count = lax.axis_size("tp")
    tp_index = lax.axis_index("tp")
    rank, columns = adapter_up_maps.shape[1:]
    features = hidden.shape[1]
    slice_width = features // tp_count
    down_slice = lax.dynamic_slice_in_dim(
        adapter_down_maps[0].T, tp_index * slice_width, slice_width, 1
    )
    up_all = lax.all_gather(adapter_up_maps[0], "req", axis=0, tiled=True)
    down_all = lax.all_gather(down_slice, "req", axis=0, tiled=True)
    gathered = lax.all_gather(hidden, "tp", axis=0, tiled=True)
    seq_count = lengths.shape[0]
    token_count = gathered.shape[0]
    pad_length = token_count // seq_count
    live_mask = jnp.arange(pad_length)[None, :] < lengths[:, None]
    token_ids = jnp.repeat(request_adapter_index, pad_length)
    chosen = token_ids[:, None] == jnp.arange(owners)[None, :]
    chosen = chosen & live_mask.reshape(token_count)[:, None]
    chosen = jnp.repeat(chosen, rank, axis=1)
    token_slice = lax.dynamic_slice_in_dim(gathered, tp_index * slice_width, slice_width, 1)
    partial = lax.dot_general(
        token_slice, down_all, (((1,), (1,)), ((), ())), preferred_element_type=jnp.float32
    )
    partial = jnp.sum(jnp.where(chosen, partial, 0.0).reshape(token_count, owners, rank), axis=1)
    shrink = lax.psum(partial, "tp").astype(jnp.bfloat16)
    spread = jnp.where(chosen, jnp.tile(shrink, (1, owners)), jnp.bfloat16(0))
    delta_rows = (
        jnp.dot(spread, up_all, preferred_element_type=jnp.float32)
        .astype(jnp.bfloat16)
        .astype(jnp.float32)
    )
    gate_pre = jnp.dot(gathered, gate_weight, preferred_element_type=jnp.float32) * gate_scale
    up_pre = (
        jnp.dot(gathered, up_weight, preferred_element_type=jnp.float32) + 0.5 * delta_rows
    ) * up_scale
    hidden_units = (jax.nn.silu(gate_pre) * up_pre).astype(jnp.bfloat16)
    row_share = token_count // tp_count
    row_start = tp_index * row_share
    branch = lax.psum_scatter(
        jnp.dot(hidden_units, down_weight, preferred_element_type=jnp.float32),
        "tp",
        scatter_dimension=0,
        tiled=True,
    )
    start_state = rms_norm(hidden.astype(jnp.float32))
    blended = start_state + update_step_size * (rms_norm(branch) - start_state)
    live_rows = lax.dynamic_slice_in_dim(
        live_mask.reshape(token_count).astype(jnp.float32), row_start, row_share, 0
    )
    return (rms_norm(blended) * live_rows[:, None]).astype(jnp.bfloat16)


def solution(mesh):
    placed = (
        P(("req", "tp"), None),
        P(None, "tp"),
        P(None, "tp"),
        P("tp", None),
        P("tp"),
        P("tp"),
        P(),
        P("req", None, None),
        P("req", None, "tp"),
        P("req"),
        P("req"),
    )
    return jax.shard_map(
        body, mesh=mesh, in_specs=placed, out_specs=P(("req", "tp"), None), check_vma=False
    )
```

time: 276 us -> 204 us (0.74)
  waiting for transfers between devices: 81.9 us -> 42.8 us
  blocking collectives: 153 us -> 134 us
  starting transfers between devices: 7.73 us -> 0.04 us
  matrix products: 8.58 us -> 5.22 us
    all_to_all x1 -> x0, blocking collectives: 133 us -> none  [body(): lax.all_to_all(outgoing, 'req', split_axis=0, concat_axis=0, tiled=True)]
    all_gather x0 -> x1, blocking collectives: none -> 83.8 us  [body(): down_all = lax.all_gather(down_slice, 'req', axis=0, tiled=True)]
    all_to_all x1 -> x0, waiting for transfers between devices: 48.1 us -> none  [body(): lax.all_to_all(delta, 'req', split_axis=0, concat_axis=0, tiled=True)]
    all_gather x1, blocking collectives: 19.8 us -> 37.9 us  [body(): gathered = lax.all_gather(hidden, 'tp', axis=0, tiled=True)]
    psum x0 -> x1, blocking collectives: none -> 12.2 us  [body(): shrink = lax.psum(partial, 'tp').astype(jnp.bfloat16)]
    reduce_scatter x1, waiting for transfers between devices: 33.8 us -> 42.1 us  [body(): lax.psum_scatter(jnp.dot(hidden_units, down_weight, preferred_element_typ...]
    all_to_all x1 -> x0, starting transfers between devices: 7.69 us -> none  [body(): lax.all_to_all(delta, 'req', split_axis=0, concat_axis=0, tiled=True)]
    convert_element_type x4 -> x0, local copies, waits for them, and re-layouts: 3.17 us -> none  [the longest x1 1.57 us: body(): delta = jnp.einsum('sjr,rf->sjf', shrink, request_up_map, preferred_eleme...]
  transfers between devices with their start and end apart: 2 -> 2, of which waited for: 2 -> 1; matrix products, arithmetic and copies ran while one was open for 1% -> 3% of each run, Pallas kernels for 0% -> 0%
where the time goes in v1:
time: 204 us; the launch traced here: 203 us
  blocking collectives  134 us (66%)
  waiting for transfers between devices  42.8 us (21%)
  between operations  13.6 us (7%)
  other arithmetic  5.44 us (3%)
  matrix products  5.22 us (3%)
  local copies, waits for them, and re-layouts  2.23 us (1%)
    all_gather x1, blocking collectives, body(): down_all = lax.all_gather(down_slice, 'req', axis=0, tiled=True)  83.8 us
    reduce_scatter x1, waiting for transfers between devices, body(): lax.psum_scatter(jnp.dot(hidden_units, down_weight, preferred_element_typ...  42.1 us
    all_gather x1, blocking collectives, body(): gathered = lax.all_gather(hidden, 'tp', axis=0, tiled=True)  37.9 us
    psum x1, blocking collectives, body(): shrink = lax.psum(partial, 'tp').astype(jnp.bfloat16)  12.2 us
  transfers between devices with their start and end apart: 2, of which 1 were waited for; matrix products, arithmetic and copies ran while one was open for 3% of the time, Pallas kernels for 0%

profile of v1, /device:TPU:1, one launch (start us, length us, event | category | flops | bytes accessed | tf_op | source)
XLA Modules:
  0.0 203.3 jit_solution(6670326683460423304)
XLA Ops:
  6.5 0.0 copy-start
  6.5 0.0 all-gather.3.cloned.1.call-start
  6.5 0.7 all-gather.3.cloned.1.call-update
  7.3 0.0 reduce-scatter.2.cloned.1.call-start
  7.3 0.7 iota_compare_fusion.1
  8.0 0.1 lt.31
  8.1 0.7 broadcast_in_dim.12
  8.9 0.1 eq.15
  9.0 0.2 copy.12
  9.2 0.8 dynamic-slice_bitcast_fusion
  10.0 83.8 %all_gather.10 = bf16[1024,160]{1,0:T(8,128)(2,1)S(1)} all-gather(bf16[16,160]{1,0:T(8,128)(2,1)S(1)} %dynamic-slice_bitcast_fusion), channel_id=1, replica_groups=mesh['req'=64,'tp'=8] {'req'}, dimensions={0}, use_global_device_ids=true | all-gather | bytes 332800 | tf_op jit(solution)/shard_map/all_gather | solution.py:34
  93.8 37.9 %all_gather.9 = bf16[128,1280]{1,0:T(8,128)(2,1)S(1)} all-gather(bf16[16,1280]{1,0:T(8,128)(2,1)} %param.11), channel_id=1, replica_groups=mesh['req'=64,'tp'=8] {'tp'}, dimensions={0}, use_global_device_ids=true | all-gather | bytes 368640 | tf_op jit(solution)/shard_map/all_gather | solution.py:35
  131.8 0.0 copy-start.5
  131.8 0.3 convolution_select_fusion
  132.1 0.2 copy.13
  132.3 0.1 reduce_sum.37
  132.4 12.2 %psum.7 = bf16[128,16]{0,1:T(8,128)(2,1)S(1)} all-reduce(f32[128,16]{0,1:T(8,128)S(1)} %reduce_sum.37), channel_id=1, replica_groups=mesh['req'=64,'tp'=8] {'tp'}, use_global_device_ids=true, to_apply=%region_2.3 | all-reduce | flops 2048 | bytes 12288 | tf_op jit(solution)/shard_map/psum | solution.py:49
  144.6 0.8 bitcast_select_fusion
  145.4 0.0 copy-done.5
  145.4 0.0 copy-start.1
  145.4 0.0 copy-start.4
  145.4 1.8 convolution_multiply_fusion
  147.2 0.0 all-gather.3.cloned.1.call-done
  147.2 1.6 fusion.4
  148.8 0.0 copy-done
  148.8 0.0 copy-done.1
  148.9 0.0 copy-done.4
  148.9 0.0 copy-start.2
  148.9 0.0 copy-start.3
  148.9 1.5 fusion.5
  150.4 0.0 reduce-scatter.2.cloned.1.call-update
  150.4 0.1 dynamic_slice.11
  150.5 0.0 copy-done.2
  150.5 0.1 fusion.17
  150.6 42.1 %reduce-scatter.2.cloned.1.call-done = f32[16,1280]{1,0:T(8,128)} async-done(((f32[128,1280]{1,0:T(8,128)}), f32[16,1280]{1,0:T(8,128)}) %reduce-scatter.2.cloned.1.call-update) | async-done | bytes 81936 | tf_op jit(solution)/shard_map/reduce_scatter | solution.py:63
  192.7 1.0 multiply_reduce_fusion.1
  193.7 0.0 copy-done.3
  193.7 1.1 multiply_reduce_fusion
  194.8 1.6 multiply_convert_fusion
  (6 shorter events, 0.1 us)
Async XLA Ops:
  6.5 142.3 %copy-start = (bf16[512,1280]{1,0:T(8,128)(2,1)S(1)}, bf16[512,1280]{1,0:T(8,128)(2,1)}, u32[]{:S(2)}) copy-start(bf16[512,1280]{1,0:T(8,128)(2,1)} %param.14) | copy-start | bytes 3932164
  6.5 140.6 %all-gather.3.cloned.1.call-start = ((), (), s32[]{:S(2)}) async-start(), calls=%async_computation.2 | async-start | bytes 1064960 | tf_op jit(solution)/shard_map/all_gather | solution.py:33
  7.3 185.4 %reduce-scatter.2.cloned.1.call-start = ((), (), s32[]{:S(2)}) async-start(), calls=%async_computation.1 | async-start | bytes 737280 | tf_op jit(solution)/shard_map/reduce_scatter | solution.py:63
  131.8 13.6 %copy-start.5 = (f32[512]{0:T(512)S(1)}, f32[512]{0:T(512)}, u32[]{:S(2)}) copy-start(f32[512]{0:T(512)} %param.15) | copy-start | bytes 6148
  145.4 3.5 %copy-start.1 = (bf16[1280,512]{1,0:T(8,128)(2,1)S(1)}, bf16[1280,512]{1,0:T(8,128)(2,1)}, u32[]{:S(2)}) copy-start(bf16[1280,512]{1,0:T(8,128)(2,1)} %param.13) | copy-start | bytes 3932164
  145.4 3.5 %copy-start.4 = (f32[512]{0:T(512)S(1)}, f32[512]{0:T(512)}, u32[]{:S(2)}) copy-start(f32[512]{0:T(512)} %param.16) | copy-start | bytes 6148
  148.9 1.6 copy-start.2
  148.9 44.8 %copy-start.3 = (f32[1280]{0:T(1024)S(1)}, f32[1280]{0:T(1024)}, u32[]{:S(2)}) copy-start(f32[1280]{0:T(1024)} %param.17) | copy-start | bytes 15364
Sparse Core Ops, SparseCore 0:
  10.3 135.0 all-gather.2
  150.5 42.1 reduce-scatter.1

commit v2 on v1

v2 whole, which is shorter than its diff:
```python
import functools

import jax
import jax.numpy as jnp
from jax import lax
from jax.experimental import pallas as pl
from jax.experimental.pallas import tpu as pltpu
from jax.sharding import PartitionSpec as P

MESH = pl.DeviceIdType.MESH
NX, NZ = 4, 16
EPS = 1e-06


def rms_norm(values):
    return values * lax.rsqrt(jnp.mean(values * values, axis=-1, keepdims=True) + EPS)


def kernel(
    tp_count,
    hidden_ref,
    gate_hbm,
    up_hbm,
    down_hbm,
    gate_scale_ref,
    up_scale_ref,
    step_ref,
    down_map_ref,
    up_map_ref,
    lengths_ref,
    ids_ref,
    out_ref,
    tokens,
    gate_w,
    up_w,
    down_w,
    gate_pre,
    up_base,
    maps,
    sums_out,
    sums_in,
    part_out,
    part_in,
    load_sem,
    tok_send,
    tok_recv,
    map_send,
    map_recv,
    sum_send,
    sum_recv,
    part_send,
    part_recv,
):
    me_r = lax.axis_index("req")
    me_t = lax.axis_index("tp")
    x = me_r // NZ
    z = lax.rem(me_r, NZ)
    pad, features = hidden_ref.shape
    rank, columns = up_map_ref.shape
    owners = maps.shape[0]
    window = maps.shape[2] - columns
    token_count = tp_count * pad
    peers = [lax.rem(me_t + k, tp_count) for k in range(1, tp_count)]

    def at(dx, dz):
        return lax.rem(x + dx + NX, NX) * NZ + lax.rem(z + dz + NZ, NZ)

    barrier = pltpu.get_barrier_semaphore()
    for peer in peers:
        pl.semaphore_signal(barrier, inc=1, device_id=(me_r, peer), device_id_type=MESH)
    for dx, dz in ((0, 1), (0, -1), (1, 0), (-1, 0)):
        pl.semaphore_signal(barrier, inc=1, device_id=(at(dx, dz), me_t), device_id_type=MESH)

    loads = [
        pltpu.make_async_copy(source, target, load_sem.at[i])
        for i, (source, target) in enumerate(
            ((gate_hbm, gate_w), (up_hbm, up_w), (down_hbm, down_w))
        )
    ]
    for load in loads:
        load.start()

    share = features // tp_count
    start = pl.multiple_of((me_t * share) // 128 * 128, 128)
    offset = me_t * share - start
    down_part = down_map_ref[pl.ds(start, window), :].astype(jnp.float32).T
    lane = lax.broadcasted_iota(jnp.int32, (rank, window), 1)
    down_part = jnp.where((lane >= offset) & (lane < offset + share), down_part, 0.0)
    maps[me_r, :, :columns] = up_map_ref[...]
    maps[me_r, :, columns:] = down_part.astype(jnp.bfloat16)
    own_rows = pl.ds(pl.multiple_of(me_t * pad, pad), pad)
    tokens[own_rows, :] = hidden_ref[...]

    lane = lax.broadcasted_iota(jnp.int32, (1, token_count), 1)
    token_ids = jnp.full((1, token_count), -1, jnp.int32)
    for s in range(tp_count):
        inside = (lane >= s * pad) & (lane < s * pad + lengths_ref[s])
        token_ids = jnp.where(inside, ids_ref[s], token_ids)
    owner_ids = lax.broadcasted_iota(jnp.int32, (owners, 1, token_count), 0)
    chosen = owner_ids == token_ids[None]

    pl.semaphore_wait(barrier, tp_count - 1 + 4)

    def to_peers(source, target, send_sem, recv_sem):
        copies = []
        for k, peer in enumerate(peers):
            copies.append(
                pltpu.make_async_remote_copy(
                    src_ref=source(peer),
                    dst_ref=target(me_t),
                    send_sem=send_sem.at[k],
                    recv_sem=recv_sem.at[me_t],
                    device_id=(me_r, peer),
                    device_id_type=MESH,
                )
            )
            copies[-1].start()
        return copies

    def from_peers(source, target, send_sem, recv_sem):
        for k, peer in enumerate(peers):
            pltpu.make_async_remote_copy(
                src_ref=source(peer),
                dst_ref=target(peer),
                send_sem=send_sem.at[k],
                recv_sem=recv_sem.at[peer],
                device_id=(me_r, peer),
                device_id_type=MESH,
            ).wait_recv()

    map_copies = []

    def map_copy(slot, device, index):
        return pltpu.make_async_remote_copy(
            src_ref=maps.at[slot],
            dst_ref=maps.at[slot],
            send_sem=map_send.at[index],
            recv_sem=map_recv.at[slot],
            device_id=(device, me_t),
            device_id_type=MESH,
        )

    def send_map(slot, device):
        copy = map_copy(slot, device, len(map_copies))
        map_copies.append(copy)
        copy.start()

    def wait_map(slot):
        map_copy(slot, at(0, 1), 0).wait_recv()

    token_args = (
        lambda peer: hidden_ref,
        lambda t: tokens.at[pl.ds(pl.multiple_of(t * pad, pad), pad)],
        tok_send,
        tok_recv,
    )
    half = NZ // 2
    z_next, z_last, x_next, x_last = at(0, 1), at(0, -1), at(1, 0), at(-1, 0)

    def z_step(s):
        minus, plus = s <= half, 0 < s < half
        if s > 0:
            wait_map(at(0, -s))
        if s < half:
            send_map(at(0, -s), z_next)
        if plus:
            wait_map(at(0, s))
        if s < half - 1:
            send_map(at(0, s), z_last)
        for dz in ((-s, s) if plus else (-s,)):
            send_map(at(0, dz), x_next)
            send_map(at(0, dz), x_last)

    def x_step(s):
        plus = 0 < s < half
        for dz in ((-s, s) if plus else (-s,)):
            wait_map(at(-1, dz))
            if dz <= 0:
                send_map(at(-1, dz), x_next)
            wait_map(at(1, dz))
            if dz > 0:
                send_map(at(1, dz), x_last)

    z_step(0)
    token_copies = to_peers(*token_args)
    for s in range(1, half + 1):
        z_step(s)
        x_step(s - 1)
        if s == 1:
            from_peers(*token_args)
            loads[0].wait()
            gate_pre[...] = jnp.dot(tokens[...], gate_w[...], preferred_element_type=jnp.float32)
        if s == 2:
            loads[1].wait()
            up_base[...] = jnp.dot(tokens[...], up_w[...], preferred_element_type=jnp.float32)
        if s == 3:
            v = gate_pre[...] * gate_scale_ref[...]
            gate_pre[...] = v / (1.0 + jnp.exp(-v))
    x_step(half)
    for s in range(half + 1):
        for dz in ((-s, s) if 0 < s < half else (-s,)):
            wait_map(at(2, dz))

    token_share = tokens[:, pl.ds(start, window)]
    products = lax.dot_general(
        maps[:, :, columns:].reshape(owners * rank, window),
        token_share,
        (((1,), (1,)), ((), ())),
        preferred_element_type=jnp.float32,
    ).reshape(owners, rank, token_count)
    partial = jnp.sum(jnp.where(chosen, products, 0.0), axis=0)
    sums_out[...] = partial
    sum_args = (lambda peer: sums_out, lambda t: sums_in.at[t], sum_send, sum_recv)
    sum_copies = to_peers(*sum_args)
    from_peers(*sum_args)
    shrink = partial
    for peer in peers:
        shrink = shrink + sums_in[peer]
    shrink = shrink.astype(jnp.bfloat16).astype(jnp.float32)
    spread = jnp.where(chosen, shrink[None], 0.0).astype(jnp.bfloat16)
    delta = lax.dot_general(
        spread.reshape(owners * rank, token_count),
        maps[:, :, :columns].reshape(owners * rank, columns),
        (((0,), (0,)), ((), ())),
        preferred_element_type=jnp.float32,
    )
    delta = delta.astype(jnp.bfloat16).astype(jnp.float32)
    up_pre = (up_base[...] + 0.5 * delta) * up_scale_ref[...]
    inner = (gate_pre[...] * up_pre).astype(jnp.bfloat16)
    loads[2].wait()
    gate_rows = jnp.dot(inner, down_w[...], preferred_element_type=jnp.float32)
    part_out[...] = gate_rows.astype(jnp.bfloat16).reshape(tp_count, pad, features)
    part_args = (lambda peer: part_out.at[peer], lambda t: part_in.at[t], part_send, part_recv)
    part_copies = to_peers(*part_args)

    begin = rms_norm(hidden_ref[...].astype(jnp.float32))
    branch = part_out[me_t].astype(jnp.float32)
    from_peers(*part_args)
    for peer in peers:
        branch = branch + part_in[peer].astype(jnp.float32)
    mixed = begin + step_ref[...] * (rms_norm(branch) - begin)
    row = lax.broadcasted_iota(jnp.int32, (pad, features), 0)
    out_ref[...] = jnp.where(row < lengths_ref[me_t], rms_norm(mixed), 0.0).astype(jnp.bfloat16)
    for copy in token_copies + sum_copies + part_copies + map_copies:
        copy.wait_send()


def body(
    hidden,
    gate_weight,
    up_weight,
    down_weight,
    gate_scale,
    up_scale,
    update_step_size,
    adapter_down_maps,
    adapter_up_maps,
    lengths,
    request_adapter_index,
):
    tp_count = lax.axis_size("tp")
    owners = lax.axis_size("req")
    pad, features = hidden.shape
    rank, columns = adapter_up_maps.shape[1:]
    token_count = tp_count * pad
    bf16, f32 = jnp.bfloat16, jnp.float32
    vmem = pl.BlockSpec(memory_space=pltpu.VMEM)
    smem = pl.BlockSpec(memory_space=pltpu.SMEM)
    hbm = pl.BlockSpec(memory_space=pl.ANY)
    dma = pltpu.SemaphoreType.DMA
    return pl.pallas_call(
        functools.partial(kernel, tp_count),
        out_shape=jax.ShapeDtypeStruct((pad, features), bf16),
        in_specs=[vmem, hbm, hbm, hbm, vmem, vmem, vmem, vmem, vmem, smem, smem],
        out_specs=vmem,
        scratch_shapes=[
            pltpu.VMEM((token_count, features), bf16),
            pltpu.VMEM(gate_weight.shape, bf16),
            pltpu.VMEM(up_weight.shape, bf16),
            pltpu.VMEM(down_weight.shape, bf16),
            pltpu.VMEM((token_count, columns), f32),
            pltpu.VMEM((token_count, columns), f32),
            pltpu.VMEM((owners, rank, columns + 256), bf16),
            pltpu.VMEM((rank, token_count), f32),
            pltpu.VMEM((tp_count, rank, token_count), f32),
            pltpu.VMEM((tp_count, pad, features), bf16),
            pltpu.VMEM((tp_count, pad, features), bf16),
            dma((3,)),
            dma((tp_count - 1,)),
            dma((tp_count,)),
            dma((owners - 1,)),
            dma((owners,)),
            dma((tp_count - 1,)),
            dma((tp_count,)),
            dma((tp_count - 1,)),
            dma((tp_count,)),
        ],
        compiler_params=pltpu.CompilerParams(
            collective_id=0, has_side_effects=True, vmem_limit_bytes=40 * 1024 * 1024
        ),
    )(
        hidden,
        gate_weight,
        up_weight,
        down_weight,
        gate_scale[None],
        up_scale[None],
        update_step_size[None],
        adapter_down_maps[0],
        adapter_up_maps[0],
        lengths,
        request_adapter_index,
    )


def solution(mesh):
    placed = (
        P(("req", "tp"), None),
        P(None, "tp"),
        P(None, "tp"),
        P("tp", None),
        P("tp"),
        P("tp"),
        P(),
        P("req", None, None),
        P("req", None, "tp"),
        P("req"),
        P("req"),
    )
    return jax.shard_map(
        body, mesh=mesh, in_specs=placed, out_specs=P(("req", "tp"), None), check_vma=False
    )
```

time: 204 us -> 68.7 us (0.34)
  blocking collectives: 134 us -> 0 us
  Pallas kernels: 0 us -> 57.8 us
  waiting for transfers between devices: 42.8 us -> 0 us
  between operations: 13.6 us -> 0.03 us
  local copies, waits for them, and re-layouts: 2.23 us -> 10.4 us
  other arithmetic: 5.44 us -> 0 us
  matrix products: 5.22 us -> 0 us
    all_gather x2 -> x0, blocking collectives: 122 us -> none  [the longest x1 83.8 us: body(): down_all = lax.all_gather(down_slice, 'req', axis=0, tiled=True)]
    pallas_call x0 -> x1, Pallas kernels: none -> 57.8 us  [body(): pl.pallas_call(functools.partial(kernel, tp_count), out_shape=jax.ShapeDt...]
    reduce_scatter x1 -> x0, waiting for transfers between devices: 42.1 us -> none  [body(): lax.psum_scatter(jnp.dot(hidden_units, down_weight, preferred_element_typ...]
    psum x1 -> x0, blocking collectives: 12.2 us -> none  [body(): shrink = lax.psum(partial, 'tp').astype(jnp.bfloat16)]
    unnamed x12 -> x20, local copies, waits for them, and re-layouts: 0.03 us -> 9.73 us
    dot_general x4 -> x0, matrix products: 5.22 us -> none  [the longest x1 1.76 us: body(): jnp.dot(gathered, gate_weight, preferred_element_type=jnp.float32)]
    reduce_sum x4 -> x0, other arithmetic: 2.29 us -> none  [the longest x3 2.22 us: rms_norm(): jnp.mean(values * values, axis=-1, keepdims=True) + 1e-06]
  transfers between devices with their start and end apart: 2 -> 0, of which waited for: 1 -> 0; matrix products, arithmetic and copies ran while one was open for 3% -> 0% of each run, Pallas kernels for 0% -> 0%
where the time goes in v2:
time: 68.7 us; the launch traced here: 68.2 us
  Pallas kernels  57.8 us (84%)
  local copies, waits for them, and re-layouts  10.4 us (15%)
    pallas_call x1, Pallas kernels, body(): pl.pallas_call(functools.partial(kernel, tp_count), out_shape=jax.ShapeDt...  57.8 us
    unnamed x20, local copies, waits for them, and re-layouts  9.73 us

profile of v2, /device:TPU:1, one launch (start us, length us, event | category | flops | bytes accessed | tf_op | source)
XLA Modules:
  0.0 68.2 jit_solution(16404034212047410451)
XLA Ops:
  0.0 0.7 %broadcast_in_dim.11.step_ref = f32[1,1280]{1,0:T(1,128)S(1)} reshape(f32[1280]{0:T(1024)} %param.17) | data formatting | bytes 10240 | tf_op jit(solution)/shard_map/broadcast_in_dim | solution.py:308
  0.7 1.0 %copy.12 = bf16[1,1280,16]{2,1,0:T(8,128)(2,1)S(1)} copy(bf16[1,1280,16]{1,2,0:T(8,128)(2,1)} %param.18) | data formatting | bytes 81920 | tf_op args[7]
  1.7 0.0 copy-start
  1.7 1.3 %copy-done = bf16[1280,512]{1,0:T(8,128)(2,1)S(1)} copy-done((bf16[1280,512]{1,0:T(8,128)(2,1)S(1)}, bf16[1280,512]{1,0:T(8,128)(2,1)}, u32[]{:S(2)}) %copy-start) | copy-done | bytes 1310744
  3.0 0.0 copy-start.1
  3.0 1.3 %copy-done.1 = bf16[1280,512]{1,0:T(8,128)(2,1)S(1)} copy-done((bf16[1280,512]{1,0:T(8,128)(2,1)S(1)}, bf16[1280,512]{1,0:T(8,128)(2,1)}, u32[]{:S(2)}) %copy-start.1) | copy-done | bytes 1310744
  4.3 0.0 copy-start.2
  4.3 1.3 %copy-done.2 = bf16[512,1280]{1,0:T(8,128)(2,1)S(1)} copy-done((bf16[512,1280]{1,0:T(8,128)(2,1)S(1)}, bf16[512,1280]{1,0:T(8,128)(2,1)}, u32[]{:S(2)}) %copy-start.2) | copy-done | bytes 1310744
  5.7 0.0 copy-start.3
  5.7 0.8 %copy-done.3 = bf16[16,1280]{1,0:T(8,128)(2,1)S(1)} copy-done((bf16[16,1280]{1,0:T(8,128)(2,1)S(1)}, bf16[16,1280]{1,0:T(8,128)(2,1)}, u32[]{:S(2)}) %copy-start.3) | copy-done | bytes 40984
  6.4 0.0 copy-start.4
  6.4 0.7 %copy-done.4 = bf16[1,16,512]{2,1,0:T(8,128)(2,1)S(1)} copy-done((bf16[1,16,512]{2,1,0:T(8,128)(2,1)S(1)}, bf16[1,16,512]{2,1,0:T(8,128)(2,1)}, u32[]{:S(2)}) %copy-start.4) | copy-done | bytes 16408
  7.2 0.0 copy-start.5
  7.2 0.7 copy-done.5
  7.8 0.0 copy-start.6
  7.8 0.7 copy-done.6
  8.5 0.0 copy-start.7
  8.5 0.7 copy-done.7
  9.2 0.0 copy-start.8
  9.2 0.7 copy-done.8
  9.8 57.8 %shard_map.109 = bf16[16,1280]{1,0:T(8,128)(2,1)S(1)} custom-call(bf16[16,1280]{1,0:T(8,128)(2,1)S(1)} %copy-done.3, bf16[1280,512]{1,0:T(8,128)(2,1)S(1)} %copy-done, bf16[1280,512]{1,0:T(8,128)(2,1)S(1)} %copy-done.1, bf16[512,1280]{1,0:T(8,128)(2,1)S(1)} %copy-done.2, f32[1,512]{1,0:T(1,128)S(1)} %bitcast.6, f32[1,512]{1,0:T(1,128)S(1)} %bitcast.7, ...), custom_call_target="tpu_custom_call" | custom-call | tf_op jit(solution)/shard_map/pallas_call | solution.py:271
  67.6 0.6 copy.14
Async XLA Ops:
  1.7 1.3 %copy-start = (bf16[1280,512]{1,0:T(8,128)(2,1)S(1)}, bf16[1280,512]{1,0:T(8,128)(2,1)}, u32[]{:S(2)}) copy-start(bf16[1280,512]{1,0:T(8,128)(2,1)} %gate_hbm.1) | copy-start | bytes 3932164
  3.0 1.3 %copy-start.1 = (bf16[1280,512]{1,0:T(8,128)(2,1)S(1)}, bf16[1280,512]{1,0:T(8,128)(2,1)}, u32[]{:S(2)}) copy-start(bf16[1280,512]{1,0:T(8,128)(2,1)} %up_hbm.1) | copy-start | bytes 3932164
  4.3 1.3 %copy-start.2 = (bf16[512,1280]{1,0:T(8,128)(2,1)S(1)}, bf16[512,1280]{1,0:T(8,128)(2,1)}, u32[]{:S(2)}) copy-start(bf16[512,1280]{1,0:T(8,128)(2,1)} %down_hbm.1) | copy-start | bytes 3932164
  5.7 0.8 %copy-start.3 = (bf16[16,1280]{1,0:T(8,128)(2,1)S(1)}, bf16[16,1280]{1,0:T(8,128)(2,1)}, u32[]{:S(2)}) copy-start(bf16[16,1280]{1,0:T(8,128)(2,1)} %hidden_ref.1) | copy-start | bytes 122884
  6.4 0.7 %copy-start.4 = (bf16[1,16,512]{2,1,0:T(8,128)(2,1)S(1)}, bf16[1,16,512]{2,1,0:T(8,128)(2,1)}, u32[]{:S(2)}) copy-start(bf16[1,16,512]{2,1,0:T(8,128)(2,1)} %param.19) | copy-start | bytes 49156
  7.2 0.7 copy-start.5
  7.8 0.7 copy-start.6
  8.5 0.7 copy-start.7
  9.2 0.7 copy-start.8

commit v3 on v2

v3 whole, which is shorter than its diff:
```python
import functools

import jax
import jax.numpy as jnp
from jax import lax
from jax.experimental import pallas as pl
from jax.experimental.pallas import tpu as pltpu
from jax.sharding import PartitionSpec as P

MESH = pl.DeviceIdType.MESH
NX, NZ = 4, 16
STRIDE = 4
EPS = 1e-06


def rms_norm(values):
    return values * lax.rsqrt(jnp.mean(values * values, axis=-1, keepdims=True) + EPS)


def kernel(
    tp_count,
    hidden_hbm,
    gate_hbm,
    up_hbm,
    down_hbm,
    gate_scale_hbm,
    up_scale_hbm,
    step_hbm,
    down_map_hbm,
    up_map_hbm,
    lengths_hbm,
    ids_hbm,
    out_ref,
    tokens,
    gate_w,
    up_w,
    down_w,
    gate_scale_ref,
    up_scale_ref,
    step_ref,
    lengths_ref,
    ids_ref,
    gate_pre,
    up_base,
    downs,
    ups,
    sums_out,
    sums_in,
    part_out,
    part_in,
    load_sem,
    tok_send,
    tok_recv,
    down_send,
    down_recv,
    up_send,
    up_recv,
    sum_send,
    sum_recv,
    part_send,
    part_recv,
):
    me_r = lax.axis_index("req")
    me_t = lax.axis_index("tp")
    x = me_r // NZ
    z = lax.rem(me_r, NZ)
    pad, features = hidden_hbm.shape
    rank, columns = up_map_hbm.shape
    owners, _, window = downs.shape
    token_count = tp_count * pad
    peers = [lax.rem(me_t + k, tp_count) for k in range(1, tp_count)]

    def at(dx, dz):
        return lax.rem(x + dx + NX, NX) * NZ + lax.rem(z + dz + NZ, NZ)

    barrier = pltpu.get_barrier_semaphore()
    for peer in peers:
        pl.semaphore_signal(barrier, inc=1, device_id=(me_r, peer), device_id_type=MESH)
    near = [(0, sign * d) for d in range(1, STRIDE + 1) for sign in (1, -1)] + [(1, 0), (-1, 0)]
    for dx, dz in near:
        pl.semaphore_signal(barrier, inc=1, device_id=(at(dx, dz), me_t), device_id_type=MESH)

    share = features // tp_count
    start = pl.multiple_of((me_t * share) // 128 * 128, 128)
    offset = me_t * share - start
    own_rows = pl.ds(pl.multiple_of(me_t * pad, pad), pad)
    loads = [
        pltpu.make_async_copy(source, target, load_sem.at[i])
        for i, (source, target) in enumerate(
            (
                (gate_hbm, gate_w),
                (up_hbm, up_w),
                (down_hbm, down_w),
                (hidden_hbm, tokens.at[own_rows]),
                (up_map_hbm, ups.at[me_r]),
                (down_map_hbm.at[:, pl.ds(start, window)], downs.at[me_r]),
                (lengths_hbm, lengths_ref),
                (ids_hbm, ids_ref),
                (gate_scale_hbm, gate_scale_ref),
                (up_scale_hbm, up_scale_ref),
                (step_hbm, step_ref),
            )
        )
    ]
    for i in (3, 4, 5, 6, 7, 8, 9, 10, 0, 1, 2):
        loads[i].start()
    for i in (6, 7, 8, 9, 10):
        loads[i].wait()

    lane = lax.broadcasted_iota(jnp.int32, (1, token_count), 1)
    token_ids = jnp.full((1, token_count), -1, jnp.int32)
    for s in range(tp_count):
        inside = (lane >= s * pad) & (lane < s * pad + lengths_ref[s])
        token_ids = jnp.where(inside, ids_ref[s], token_ids)
    owner_ids = lax.broadcasted_iota(jnp.int32, (owners, 1, token_count), 0)
    chosen = owner_ids == token_ids[None]

    for i in (3, 4, 5):
        loads[i].wait()
    pl.semaphore_wait(barrier, tp_count - 1 + len(near))

    def to_peers(source, target, send_sem, recv_sem):
        copies = []
        for k, peer in enumerate(peers):
            copies.append(
                pltpu.make_async_remote_copy(
                    src_ref=source(peer),
                    dst_ref=target(me_t),
                    send_sem=send_sem.at[k],
                    recv_sem=recv_sem.at[me_t],
                    device_id=(me_r, peer),
                    device_id_type=MESH,
                )
            )
            copies[-1].start()
        return copies

    def from_peers(source, target, send_sem, recv_sem):
        for k, peer in enumerate(peers):
            pltpu.make_async_remote_copy(
                src_ref=source(peer),
                dst_ref=target(peer),
                send_sem=send_sem.at[k],
                recv_sem=recv_sem.at[peer],
                device_id=(me_r, peer),
                device_id_type=MESH,
            ).wait_recv()

    kinds = ((downs, down_send, down_recv, []), (ups, up_send, up_recv, []))
    down, up = kinds

    def map_copy(kind, slot, device, index):
        blocks, send_sem, recv_sem, _ = kind
        return pltpu.make_async_remote_copy(
            src_ref=blocks.at[slot],
            dst_ref=blocks.at[slot],
            send_sem=send_sem.at[index],
            recv_sem=recv_sem.at[slot],
            device_id=(device, me_t),
            device_id_type=MESH,
        )

    def send_map(kind, slot, device):
        copy = map_copy(kind, slot, device, len(kind[3]))
        kind[3].append(copy)
        copy.start()

    def wait_map(kind, slot):
        map_copy(kind, slot, at(0, 1), 0).wait_recv()

    token_args = (
        lambda peer: tokens.at[own_rows],
        lambda t: tokens.at[pl.ds(pl.multiple_of(t * pad, pad), pad)],
        tok_send,
        tok_recv,
    )
    half = NZ // 2
    x_next, x_last = at(1, 0), at(-1, 0)
    stages = -(-half // STRIDE)
    arrived = set()

    def wait_once(kind, dz):
        if dz != 0 and (id(kind), dz) not in arrived:
            arrived.add((id(kind), dz))
            wait_map(kind, at(0, dz))

    def z_send(kind, stage):
        base = stage * STRIDE
        for sign, reach in ((1, half), (-1, half - 1)):
            steps = range(min(base + STRIDE, reach), base, -1)
            if len(steps):
                wait_once(kind, -sign * base)
            for to in steps:
                send_map(kind, at(0, -sign * base), at(0, sign * (to - base)))

    def members(stage):
        if stage == 0:
            return [0]
        near = range((stage - 1) * STRIDE + 1, min(stage * STRIDE, half) + 1)
        return [dz for d in near for dz in ((-d, d) if d < half else (-d,))]

    def x_send(kind, stage):
        for dz in members(stage):
            wait_once(kind, dz)
            send_map(kind, at(0, dz), x_next)
            send_map(kind, at(0, dz), x_last)

    def x_pass(kind, stage):
        for dz in members(stage):
            wait_map(kind, at(-1, dz))
            if dz <= 0:
                send_map(kind, at(-1, dz), x_next)
            wait_map(kind, at(1, dz))
            if dz > 0:
                send_map(kind, at(1, dz), x_last)

    def x_finish(kind):
        for stage in range(stages + 1):
            for dz in members(stage):
                wait_map(kind, at(2, dz))

    for kind in kinds:
        z_send(kind, 0)
    token_copies = to_peers(*token_args)
    for kind in kinds:
        x_send(kind, 0)
    for stage in range(1, stages + 1):
        for kind in kinds:
            z_send(kind, stage)
        for kind in kinds:
            x_send(kind, stage)
        if stage == stages:
            break
        for kind in kinds:
            x_pass(kind, stage - 1)
        if stage == stages - 1:
            from_peers(*token_args)
            loads[0].wait()
            v = jnp.dot(tokens[...], gate_w[...], preferred_element_type=jnp.float32)
            v = v * gate_scale_ref[...][None]
            gate_pre[...] = v / (1.0 + jnp.exp(-v))
            loads[1].wait()
            up_base[...] = jnp.dot(tokens[...], up_w[...], preferred_element_type=jnp.float32)
    for stage in (stages - 1, stages):
        x_pass(down, stage)
    x_pass(up, stages - 1)
    x_finish(down)

    lane = lax.broadcasted_iota(jnp.int32, (token_count, window), 1)
    token_share = tokens[:, pl.ds(start, window)].astype(jnp.float32)
    token_share = jnp.where((lane >= offset) & (lane < offset + share), token_share, 0.0)
    token_share = token_share.astype(jnp.bfloat16)
    products = lax.dot_general(
        downs[...].reshape(owners * rank, window),
        token_share,
        (((1,), (1,)), ((), ())),
        preferred_element_type=jnp.float32,
    ).reshape(owners, rank, token_count)
    partial = jnp.sum(jnp.where(chosen, products, 0.0), axis=0)
    sums_out[...] = partial
    sum_args = (lambda peer: sums_out, lambda t: sums_in.at[t], sum_send, sum_recv)
    sum_copies = to_peers(*sum_args)
    x_pass(up, stages)
    x_finish(up)
    from_peers(*sum_args)
    shrink = partial
    for peer in peers:
        shrink = shrink + sums_in[peer]
    shrink = shrink.astype(jnp.bfloat16).astype(jnp.float32)
    spread = jnp.where(chosen, shrink[None], 0.0).astype(jnp.bfloat16)
    delta = lax.dot_general(
        spread.reshape(owners * rank, token_count),
        ups[...].reshape(owners * rank, columns),
        (((0,), (0,)), ((), ())),
        preferred_element_type=jnp.float32,
    )
    delta = delta.astype(jnp.bfloat16).astype(jnp.float32)
    up_pre = (up_base[...] + 0.5 * delta) * up_scale_ref[...][None]
    inner = (gate_pre[...] * up_pre).astype(jnp.bfloat16)
    loads[2].wait()
    gate_rows = jnp.dot(inner, down_w[...], preferred_element_type=jnp.float32)
    part_out[...] = gate_rows.astype(jnp.bfloat16).reshape(tp_count, pad, features)
    part_args = (lambda peer: part_out.at[peer], lambda t: part_in.at[t], part_send, part_recv)
    part_copies = to_peers(*part_args)

    begin = rms_norm(tokens[own_rows, :].astype(jnp.float32))
    branch = part_out[me_t].astype(jnp.float32)
    from_peers(*part_args)
    for peer in peers:
        branch = branch + part_in[peer].astype(jnp.float32)
    mixed = begin + step_ref[...][None] * (rms_norm(branch) - begin)
    row = lax.broadcasted_iota(jnp.int32, (pad, features), 0)
    out_ref[...] = jnp.where(row < lengths_ref[me_t], rms_norm(mixed), 0.0).astype(jnp.bfloat16)
    for copy in token_copies + sum_copies + part_copies + down[3] + up[3]:
        copy.wait_send()


def body(
    hidden,
    gate_weight,
    up_weight,
    down_weight,
    gate_scale,
    up_scale,
    update_step_size,
    adapter_down_maps,
    adapter_up_maps,
    lengths,
    request_adapter_index,
):
    tp_count = lax.axis_size("tp")
    owners = lax.axis_size("req")
    pad, features = hidden.shape
    rank, columns = adapter_up_maps.shape[1:]
    token_count = tp_count * pad
    bf16, f32 = jnp.bfloat16, jnp.float32
    vmem = pl.BlockSpec(memory_space=pltpu.VMEM)
    hbm = pl.BlockSpec(memory_space=pl.ANY)
    dma = pltpu.SemaphoreType.DMA
    return pl.pallas_call(
        functools.partial(kernel, tp_count),
        out_shape=jax.ShapeDtypeStruct((pad, features), bf16),
        in_specs=[hbm] * 11,
        out_specs=vmem,
        scratch_shapes=[
            pltpu.VMEM((token_count, features), bf16),
            pltpu.VMEM(gate_weight.shape, bf16),
            pltpu.VMEM(up_weight.shape, bf16),
            pltpu.VMEM(down_weight.shape, bf16),
            pltpu.VMEM(gate_scale.shape, f32),
            pltpu.VMEM(up_scale.shape, f32),
            pltpu.VMEM(update_step_size.shape, f32),
            pltpu.SMEM(lengths.shape, jnp.int32),
            pltpu.SMEM(lengths.shape, jnp.int32),
            pltpu.VMEM((token_count, columns), f32),
            pltpu.VMEM((token_count, columns), f32),
            pltpu.VMEM((owners, rank, 256), bf16),
            pltpu.VMEM((owners, rank, columns), bf16),
            pltpu.VMEM((rank, token_count), f32),
            pltpu.VMEM((tp_count, rank, token_count), f32),
            pltpu.VMEM((tp_count, pad, features), bf16),
            pltpu.VMEM((tp_count, pad, features), bf16),
            dma((11,)),
            dma((tp_count - 1,)),
            dma((tp_count,)),
            dma((owners - 1,)),
            dma((owners,)),
            dma((owners - 1,)),
            dma((owners,)),
            dma((tp_count - 1,)),
            dma((tp_count,)),
            dma((tp_count - 1,)),
            dma((tp_count,)),
        ],
        compiler_params=pltpu.CompilerParams(
            collective_id=0, has_side_effects=True, vmem_limit_bytes=67000000
        ),
    )(
        hidden,
        gate_weight,
        up_weight,
        down_weight,
        gate_scale,
        up_scale,
        update_step_size,
        adapter_down_maps.transpose(0, 2, 1)[0],
        adapter_up_maps[0],
        lengths,
        request_adapter_index,
    )


def solution(mesh):
    placed = (
        P(("req", "tp"), None),
        P(None, "tp"),
        P(None, "tp"),
        P("tp", None),
        P("tp"),
        P("tp"),
        P(),
        P("req", None, None),
        P("req", None, "tp"),
        P("req"),
        P("req"),
    )
    return jax.shard_map(
        body, mesh=mesh, in_specs=placed, out_specs=P(("req", "tp"), None), check_vma=False
    )
```

time: 68.7 us -> 50.5 us (0.74)
  local copies, waits for them, and re-layouts: 10.4 us -> 1.4 us
  Pallas kernels: 57.8 us -> 48.9 us
    pallas_call x1, Pallas kernels: 57.8 us -> 48.9 us  [body(): pl.pallas_call(functools.partial(kernel, tp_count), out_shape=jax.ShapeDt...]
    unnamed x20 -> x1, local copies, waits for them, and re-layouts: 9.73 us -> 1.4 us
    broadcast_in_dim x1 -> x0, local copies, waits for them, and re-layouts: 0.7 us -> none  [body(): update_step_size[None]]
where the time goes in v3:
time: 50.5 us; the launch traced here: 50.3 us
  Pallas kernels  48.9 us (97%)
  local copies, waits for them, and re-layouts  1.4 us (3%)
    pallas_call x1, Pallas kernels, body(): pl.pallas_call(functools.partial(kernel, tp_count), out_shape=jax.ShapeDt...  48.9 us
    unnamed x1, local copies, waits for them, and re-layouts  1.4 us

profile of v3, /device:TPU:1, one launch (start us, length us, event | category | flops | bytes accessed | tf_op | source)
XLA Modules:
  0.0 50.3 jit_solution(88630506430863395)
XLA Ops:
  0.0 48.9 %shard_map.109 = bf16[16,1280]{1,0:T(8,128)(2,1)} custom-call(bf16[16,1280]{1,0:T(8,128)(2,1)} %hidden_hbm.1, bf16[1280,512]{1,0:T(8,128)(2,1)} %gate_hbm.1, bf16[1280,512]{1,0:T(8,128)(2,1)} %up_hbm.1, bf16[512,1280]{1,0:T(8,128)(2,1)} %down_hbm.1, f32[512]{0:T(512)} %gate_scale_hbm.1, f32[512]{0:T(512)} %up_scale_hbm.1, f32[1280]{0:T(1024)} %step_hbm.1, ...), custom_call_target="tpu_custom_call" | custom-call | tf_op jit(solution)/shard_map/pallas_call | solution.py:320
  48.9 1.4 %copy.13 = bf16[16,1280]{1,0:T(8,128)(2,1)} copy(bf16[16,1280]{1,0:T(8,128)(2,1)} %shard_map.109) | data formatting | bytes 81920

commit v4 on v3

--- a/solution.py
+++ b/solution.py
@@ -9,7 +9,7 @@
 
 MESH = pl.DeviceIdType.MESH
 NX, NZ = 4, 16
-STRIDE = 4
+STRIDE = 2
 EPS = 1e-06
 
 
@@ -68,7 +68,9 @@
     rank, columns = up_map_hbm.shape
     owners, _, window = downs.shape
     token_count = tp_count * pad
-    peers = [lax.rem(me_t + k, tp_count) for k in range(1, tp_count)]
+    y, core = me_t // 2, lax.rem(me_t, 2)
+    hops = [(dy, other) for dy in (2, 1, 3) for other in (0, 1)] + [(0, 1)]
+    peers = [lax.rem(y + dy, tp_count // 2) * 2 + lax.rem(core + other, 2) for dy, other in hops]
 
     def at(dx, dz):
         return lax.rem(x + dx + NX, NX) * NZ + lax.rem(z + dz + NZ, NZ)
@@ -76,7 +78,7 @@
     barrier = pltpu.get_barrier_semaphore()
     for peer in peers:
         pl.semaphore_signal(barrier, inc=1, device_id=(me_r, peer), device_id_type=MESH)
-    near = [(0, sign * d) for d in range(1, STRIDE + 1) for sign in (1, -1)] + [(1, 0), (-1, 0)]
+    near = [(0, sign * d) for d in range(1, STRIDE + 1) for sign in (1, -1)] + [(1, 0), (-1, 0), (2, 0)]
     for dx, dz in near:
         pl.semaphore_signal(barrier, inc=1, device_id=(at(dx, dz), me_t), device_id_type=MESH)
 
@@ -202,16 +204,18 @@
     def x_send(kind, stage):
         for dz in members(stage):
             wait_once(kind, dz)
+            if kind is down:
+                send_map(kind, at(0, dz), at(2, 0))
             send_map(kind, at(0, dz), x_next)
             send_map(kind, at(0, dz), x_last)
 
     def x_pass(kind, stage):
         for dz in members(stage):
             wait_map(kind, at(-1, dz))
-            if dz <= 0:
+            if kind is up and dz <= 0:
                 send_map(kind, at(-1, dz), x_next)
             wait_map(kind, at(1, dz))
-            if dz > 0:
+            if kind is up and dz > 0:
                 send_map(kind, at(1, dz), x_last)
 
     def x_finish(kind):

time: 50.5 us -> 48.6 us (0.962)
  Pallas kernels: 48.9 us -> 47 us
    pallas_call x1, Pallas kernels: 48.9 us -> 47 us  [body(): pl.pallas_call(functools.partial(kernel, tp_count), out_shape=jax.ShapeDt...]
where the time goes in v4:
time: 48.6 us; the launch traced here: 48.4 us
  Pallas kernels  47 us (97%)
  local copies, waits for them, and re-layouts  1.4 us (3%)
    pallas_call x1, Pallas kernels, body(): pl.pallas_call(functools.partial(kernel, tp_count), out_shape=jax.ShapeDt...  47 us
    unnamed x1, local copies, waits for them, and re-layouts  1.4 us

profile of v4, /device:TPU:1, one launch (start us, length us, event | category | flops | bytes accessed | tf_op | source)
XLA Modules:
  0.0 48.4 jit_solution(10368013881783529243)
XLA Ops:
  0.0 47.0 %shard_map.109 = bf16[16,1280]{1,0:T(8,128)(2,1)} custom-call(bf16[16,1280]{1,0:T(8,128)(2,1)} %hidden_hbm.1, bf16[1280,512]{1,0:T(8,128)(2,1)} %gate_hbm.1, bf16[1280,512]{1,0:T(8,128)(2,1)} %up_hbm.1, bf16[512,1280]{1,0:T(8,128)(2,1)} %down_hbm.1, f32[512]{0:T(512)} %gate_scale_hbm.1, f32[512]{0:T(512)} %up_scale_hbm.1, f32[1280]{0:T(1024)} %step_hbm.1, ...), custom_call_target="tpu_custom_call" | custom-call | tf_op jit(solution)/shard_map/pallas_call | solution.py:324
  47.0 1.4 %copy.13 = bf16[16,1280]{1,0:T(8,128)(2,1)} copy(bf16[16,1280]{1,0:T(8,128)(2,1)} %shard_map.109) | data formatting | bytes 81920

commit v5 on v4

--- a/solution.py
+++ b/solution.py
@@ -243,8 +243,6 @@
             v = jnp.dot(tokens[...], gate_w[...], preferred_element_type=jnp.float32)
             v = v * gate_scale_ref[...][None]
             gate_pre[...] = v / (1.0 + jnp.exp(-v))
-            loads[1].wait()
-            up_base[...] = jnp.dot(tokens[...], up_w[...], preferred_element_type=jnp.float32)
     for stage in (stages - 1, stages):
         x_pass(down, stage)
     x_pass(up, stages - 1)
@@ -265,6 +263,8 @@
     sum_args = (lambda peer: sums_out, lambda t: sums_in.at[t], sum_send, sum_recv)
     sum_copies = to_peers(*sum_args)
     x_pass(up, stages)
+    loads[1].wait()
+    up_base[...] = jnp.dot(tokens[...], up_w[...], preferred_element_type=jnp.float32)
     x_finish(up)
     from_peers(*sum_args)
     shrink = partial

time: 48.6 us -> 48.4 us (level)
  no operation moved by 1% of the time
where the time goes in v5:
time: 48.4 us; the launch traced here: 48.3 us
  Pallas kernels  46.9 us (97%)
  local copies, waits for them, and re-layouts  1.4 us (3%)
    pallas_call x1, Pallas kernels, body(): pl.pallas_call(functools.partial(kernel, tp_count), out_shape=jax.ShapeDt...  46.9 us
    unnamed x1, local copies, waits for them, and re-layouts  1.4 us

profile of v5, /device:TPU:1, one launch (start us, length us, event | category | flops | bytes accessed | tf_op | source)
XLA Modules:
  0.0 48.3 jit_solution(16644181225361835185)
XLA Ops:
  0.0 46.9 %shard_map.109 = bf16[16,1280]{1,0:T(8,128)(2,1)} custom-call(bf16[16,1280]{1,0:T(8,128)(2,1)} %hidden_hbm.1, bf16[1280,512]{1,0:T(8,128)(2,1)} %gate_hbm.1, bf16[1280,512]{1,0:T(8,128)(2,1)} %up_hbm.1, bf16[512,1280]{1,0:T(8,128)(2,1)} %down_hbm.1, f32[512]{0:T(512)} %gate_scale_hbm.1, f32[512]{0:T(512)} %up_scale_hbm.1, f32[1280]{0:T(1024)} %step_hbm.1, ...), custom_call_target="tpu_custom_call" | custom-call | tf_op jit(solution)/shard_map/pallas_call | solution.py:324
  46.9 1.4 %copy.13 = bf16[16,1280]{1,0:T(8,128)(2,1)} copy(bf16[16,1280]{1,0:T(8,128)(2,1)} %shard_map.109) | data formatting | bytes 81920
